TPU v7x, 128 devices: a whole 4x4x4 slice. The times are simulated.
128 devices in a mesh: dp: 16 (over z, x), expert: 8 (over y, core).
Axes of the slice: x: 4, y: 4, z: 4, core: 2. Of those that a mesh axis runs over, the one named last changes fastest.
Arguments:
- tokens: bfloat16 [16384, 1280], P(('dp', 'expert')), may hold values from -6 to 6
- routes: int32 [16384, 2], P(('dp', 'expert')), may hold values from 0 to 31, all different within a row; in each aligned block of 128 rows (0 to 127, 128 to 255, ...) at most 10 rows name the same one
- combine: float32 [16384, 2], P(('dp', 'expert')), may hold values from 0.1 to 1
- w_in: bfloat16 [1280, 163840], P(None, ('dp', 'expert')), may hold values from -0.15625 to 0.15625
- w_out: bfloat16 [163840, 1280], P(('dp', 'expert')), may hold values from -0.078125 to 0.078125
- out_grad: bfloat16 [16384, 1280], P(('dp', 'expert')), may hold values from -6 to 6
- head_w: bfloat16 [1280, 17408], P(None, 'expert'), may hold values from -0.5 to 0.5
- labels: int32 [64, 4], P('dp'), may hold values from 0 to 17407
Outputs:
- mixed_out: bfloat16 [16384, 1280], P(('dp', 'expert'))
- d_tokens: bfloat16 [16384, 1280], P(('dp', 'expert'))
- d_combine: float32 [16384, 2], P(('dp', 'expert'))
- d_w_in: bfloat16 [1280, 163840], P(None, ('dp', 'expert'))
- d_w_out: bfloat16 [163840, 1280], P(('dp', 'expert'))
- image_loss: float32 [64], P('dp')
- d_pooled: float32 [64, 1280], P('dp')
- d_head: bfloat16 [1280, 17408], P('dp', 'expert')
Inputs may be any that keep to these rules, and one draw needn't show every extreme that they name: `routes`: in the 128 rows of each device no expert is named by more than 10 rows, a bound that some block reaches; the two entries of a row differ. `labels`: entries of one image may repeat.
All inputs are finite; a program needn't handle non-finite values.
Results may differ from a plain program's by a relative error of at most 0.015.
Values may be sent and summed in bfloat16 or wider, within the bound.
No kernel may reach another device: no remote copies, remote signals or barrier semaphores. Data moves between devices by JAX's collectives and lax.ppermute only.
A program may use at most 192 MiB of HBM per device.

v0:
```python
import jax
import jax.numpy as jnp
from jax import lax
from jax.sharding import PartitionSpec as P

D = 1280
EXPERTS = 32
PATCHES = 256
CLASSES = 17408
beta_rate = 0.99
norm_eps = 1e-06


def gelu_fn(values):
    return jax.nn.gelu(values, approximate=True)


def normalize(pooled):
    center = jnp.mean(pooled, axis=1, keepdims=True)
    spread = jnp.mean(jnp.square(pooled - center), axis=1, keepdims=True)
    return (pooled - center) * lax.rsqrt(spread + norm_eps)


def weighted_focal(logit_vals, targets, class_weight):
    nll_vals = targets * jax.nn.softplus(-logit_vals) + (1.0 - targets) * jax.nn.softplus(
        logit_vals
    )
    return class_weight[None, :] * jnp.square(1.0 - jnp.exp(-nll_vals)) * nll_vals


def expert_pass(xs_rows, grad_rows, w_first, w_second):
    h_pre = jnp.dot(xs_rows, w_first, preferred_element_type=jnp.float32)
    hidden, gelu_back = jax.vjp(gelu_fn, h_pre)
    hidden_bf = hidden.astype(jnp.bfloat16)
    expert_out = jnp.dot(hidden_bf, w_second, preferred_element_type=jnp.float32)
    d_hidden = lax.dot_general(
        grad_rows, w_second, (((1,), (1,)), ((), ())), preferred_element_type=jnp.float32
    )
    d_pre = gelu_back(d_hidden)[0].astype(jnp.bfloat16)
    d_second = lax.dot_general(
        hidden_bf, grad_rows, (((0,), (0,)), ((), ())), preferred_element_type=jnp.float32
    ).astype(jnp.bfloat16)
    d_first = lax.dot_general(
        xs_rows, d_pre, (((0,), (0,)), ((), ())), preferred_element_type=jnp.float32
    ).astype(jnp.bfloat16)
    d_rows = lax.dot_general(
        d_pre, w_first, (((1,), (1,)), ((), ())), preferred_element_type=jnp.float32
    )
    return (expert_out, d_rows, d_first, d_second)


def to_experts(stacked):
    return lax.all_to_all(stacked, ("dp", "expert"), split_axis=1, concat_axis=1, tiled=True)


def to_sources(partials):
    return lax.all_to_all(partials, ("dp", "expert"), split_axis=0, concat_axis=0, tiled=True)


def shards(tokens, routes, combine, w_in, w_out, out_grad, head_w, labels):
    dp_size = lax.axis_size("dp")
    ex_size = lax.axis_size("expert")
    n_devices = dp_size * ex_size
    tok_rows = tokens.shape[0]
    capacity = 5 * tok_rows // 64
    share_count = n_devices // EXPERTS
    buffer_rows = EXPERTS * capacity
    flat_routes = routes.reshape(tok_rows * 2)
    route_hits = (flat_routes[:, None] == jnp.arange(EXPERTS, dtype=jnp.int32)[None, :]).astype(
        jnp.int32
    )
    earlier = jnp.cumsum(route_hits, axis=0) - route_hits
    slot_pos = jnp.sum(earlier * route_hits, axis=1)
    slot_index = flat_routes * capacity + slot_pos
    pair_table = (jnp.arange(buffer_rows, dtype=jnp.int32)[:, None] == slot_index[None, :]).astype(
        jnp.bfloat16
    )
    token_table = jnp.sum(pair_table.reshape(buffer_rows, tok_rows, 2), axis=2)
    pair_grad = (
        (combine[:, :, None] * out_grad.astype(jnp.float32)[:, None, :])
        .astype(jnp.bfloat16)
        .reshape(tok_rows * 2, D)
    )
    x_buf = jnp.dot(token_table, tokens, preferred_element_type=jnp.float32).astype(jnp.bfloat16)
    g_buf = jnp.dot(pair_table, pair_grad, preferred_element_type=jnp.float32).astype(jnp.bfloat16)
    stacked = jnp.stack([x_buf, g_buf]).reshape(2, EXPERTS, 1, capacity, D)
    stacked = jnp.broadcast_to(stacked, (2, EXPERTS, share_count, capacity, D)).reshape(
        2, n_devices, capacity, D
    )
    arrived = to_experts(stacked)
    xs_rows = arrived[0].reshape(n_devices * capacity, D)
    grad_rows = arrived[1].reshape(n_devices * capacity, D)
    expert_out, d_rows, d_w_in, d_w_out = expert_pass(xs_rows, grad_rows, w_in, w_out)
    back_out = to_sources(expert_out.reshape(n_devices, capacity, D))
    expert_sum = jnp.sum(back_out.reshape(EXPERTS, share_count, capacity, D), axis=1).reshape(
        buffer_rows, D
    )
    expert_vals = jnp.take(expert_sum, slot_index, axis=0).reshape(tok_rows, 2, D)
    mixed_out = (
        tokens.astype(jnp.float32) + jnp.sum(combine[:, :, None] * expert_vals, axis=1)
    ).astype(jnp.bfloat16)
    d_combine = jnp.sum(out_grad.astype(jnp.float32)[:, None, :] * expert_vals, axis=2)
    ex_index = lax.axis_index("expert")
    row_images = ex_size * tok_rows // PATCHES
    token_image = (ex_index * tok_rows + jnp.arange(tok_rows, dtype=jnp.int32)) // PATCHES
    image_table = (jnp.arange(row_images, dtype=jnp.int32)[:, None] == token_image[None, :]).astype(
        jnp.float32
    )
    pooled_part = jnp.dot(
        image_table, mixed_out.astype(jnp.float32), precision=lax.Precision.HIGHEST
    )
    class_cols = head_w.shape[1]
    class_ids = ex_index * class_cols + jnp.arange(class_cols, dtype=jnp.int32)
    targets = jnp.any(labels[:, :, None] == class_ids[None, None, :], axis=1).astype(jnp.float32)
    counts = lax.psum(jnp.sum(targets, axis=0), "dp")
    effective = (1.0 - beta_rate) / (1.0 - jnp.power(beta_rate, counts + 1.0))
    pooled_sum, effective_total = lax.psum((pooled_part, jnp.sum(effective)), "expert")
    back_parts = to_sources(d_rows.reshape(n_devices, capacity, D))
    back_sum = jnp.sum(back_parts.reshape(EXPERTS, share_count, capacity, D), axis=1).reshape(
        buffer_rows, D
    )
    expert_back = jnp.take(back_sum, slot_index, axis=0).reshape(tok_rows, 2, D)
    d_tokens = (out_grad.astype(jnp.float32) + jnp.sum(expert_back, axis=1)).astype(jnp.bfloat16)
    class_weight = effective * CLASSES / effective_total
    pooled = pooled_sum / PATCHES
    normed, norm_back = jax.vjp(normalize, pooled)
    normed_bf = normed.astype(jnp.bfloat16)
    logits = jnp.dot(normed_bf, head_w, preferred_element_type=jnp.float32)
    focal_terms, focal_back = jax.vjp(
        lambda logit_vals: weighted_focal(logit_vals, targets, class_weight), logits
    )
    d_logits = focal_back(jnp.ones_like(focal_terms))[0].astype(jnp.bfloat16)
    normed_part = lax.dot_general(
        d_logits, head_w, (((1,), (1,)), ((), ())), preferred_element_type=jnp.float32
    )
    d_normed, image_loss = lax.psum((normed_part, jnp.sum(focal_terms, axis=1)), "expert")
    d_pooled = norm_back(d_normed)[0]
    d_head = lax.psum_scatter(
        lax.dot_general(
            normed_bf, d_logits, (((0,), (0,)), ((), ())), preferred_element_type=jnp.float32
        ).astype(jnp.bfloat16),
        "dp",
        scatter_dimension=0,
        tiled=True,
    )
    return (mixed_out, d_tokens, d_combine, d_w_in, d_w_out, image_loss, d_pooled, d_head)


def solution(mesh):
    in_specs = (
        P(("dp", "expert"), None),
        P(("dp", "expert"), None),
        P(("dp", "expert"), None),
        P(None, ("dp", "expert")),
        P(("dp", "expert"), None),
        P(("dp", "expert"), None),
        P(None, "expert"),
        P("dp", None),
    )
    out_specs = (
        P(("dp", "expert"), None),
        P(("dp", "expert"), None),
        P(("dp", "expert"), None),
        P(None, ("dp", "expert")),
        P(("dp", "expert"), None),
        P("dp"),
        P("dp", None),
        P("dp", "expert"),
    )
    return jax.shard_map(shards, mesh=mesh, in_specs=in_specs, out_specs=out_specs, check_vma=False)
```

profile of v0, /device:TPU:0, one launch (start us, length us, event | category | flops | bytes accessed | tf_op | source)
XLA Modules:
  0.0 685.1 jit_solution(5458899573106623758)
XLA Ops:
  29.6 3.8 broadcast_in_dim.16
  33.5 89.6 %all_to_all.15 = bf16[2,128,10,1280]{3,0,2,1:T(2,128)(2,1)S(1)} all-to-all(bf16[2,128,10,1280]{3,0,2,1:T(2,128)(2,1)S(1)} %bitcast.42), channel_id=1, replica_groups=mesh['dp'=16,'expert'=8] {'dp','expert'}, dimensions={1} | all-to-all | bytes 13107200 | tf_op jit(solution)/shard_map/all_to_all | solution.py:53
  123.1 40.3 %slice_reduce_fusion = (bf16[128,10,1280]{2,1,0:T(8,128)(2,1)}, bf16[128,10,1280]{2,1,0:T(8,128)(2,1)}) fusion(bf16[2,128,10,1280]{3,0,2,1:T(2,128)(2,1)S(1)} %all_to_all.15), kind=kLoop, calls=%fused_computation.16 | loop fusion | bytes 13107200 | tf_op jit(solution)/shard_map/slice | solution.py:92
  163.4 7.0 %reshape_squeeze.7 = bf16[1280,1280]{1,0:T(8,128)(2,1)} reshape(bf16[128,10,1280]{2,1,0:T(8,128)(2,1)} %get-tuple-element.49) | data formatting | bytes 6553600 | tf_op jit(solution)/shard_map/reshape;squeeze | solution.py:92
  170.4 7.0 %reshape_squeeze.6 = bf16[1280,1280]{1,0:T(8,128)(2,1)} reshape(bf16[128,10,1280]{2,1,0:T(8,128)(2,1)} %get-tuple-element.50) | data formatting | bytes 6553600 | tf_op jit(solution)/shard_map/reshape;squeeze | solution.py:91
  177.4 7.6 %fusion.37 = f32[1280,1280]{1,0:T(8,128)S(1)} fusion(bf16[1280,1280]{1,0:T(8,128)(2,1)} %reshape_squeeze.7, bf16[1280,1280]{1,0:T(8,128)(2,1)} %param.15), kind=kOutput, calls=%fused_computation.102 | convolution fusion | flops 4194304000 | bytes 13107200 | tf_op jit(solution)/shard_map/dot_general | solution.py:36
  185.0 9.4 %fusion.6 = (bf16[1280,1280]{1,0:T(8,128)(2,1)S(1)}, f32[1280,1280]{1,0:T(8,128)}) fusion(f32[1280,1280]{1,0:T(8,128)S(1)} %fusion.37, bf16[1280,1280]{1,0:T(8,128)(2,1)S(1)} %copy-done.4, bf16[1280,1280]{1,0:T(8,128)(2,1)S(1)} %copy-done), kind=kOutput, calls=%fused_computation.15 | convolution fusion | flops 4227072000 | bytes 22937600 | tf_op jit(solution)/shard_map/dot_general | solution.py:32
  196.2 6.5 fusion.38
  202.8 8.6 %reshape.154 = f32[128,10,1280]{2,1,0:T(8,128)} reshape(f32[1280,1280]{1,0:T(8,128)} %fusion.38) | data formatting | bytes 13107200 | tf_op jit(solution)/shard_map/reshape | solution.py:118
  211.4 6.3 all-to-all-start.2
  217.7 11.2 %fusion.36 = f32[1280,1280]{1,0:T(8,128)} fusion(bf16[1280,1280]{1,0:T(8,128)(2,1)S(1)} %copy-done.9, f32[1280,1280]{1,0:T(8,128)} %get-tuple-element.63), kind=kOutput, calls=%fused_computation.101 | convolution fusion | flops 4209049600 | bytes 16384000 | tf_op jit(solution)/shard_map/dot_general | solution.py:35
  228.9 8.6 %reshape.150 = f32[128,10,1280]{2,1,0:T(8,128)} reshape(f32[1280,1280]{1,0:T(8,128)} %fusion.36) | data formatting | bytes 13107200 | tf_op jit(solution)/shard_map/reshape | solution.py:94
  237.5 103.3 %all-to-all-done.2 = f32[128,10,1280]{2,1,0:T(8,128)} async-done(((f32[128,10,1280]{2,1,0:T(8,128)}), f32[128,10,1280]{2,1,0:T(8,128)}, u32[]{:S(2)}, u32[]{:S(2)}) %all-to-all-start.2) | async-done | bytes 6553632 | tf_op jit(solution)/shard_map/all_to_all | solution.py:57
  340.8 10.3 %all-to-all-start.1 = ((f32[128,10,1280]{2,1,0:T(8,128)}), f32[128,10,1280]{2,1,0:T(8,128)}, u32[]{:S(2)}, u32[]{:S(2)}) async-start(f32[128,10,1280]{2,1,0:T(8,128)} %reshape.150), calls=%async_computation.1 | async-start | bytes 20971520 | tf_op jit(solution)/shard_map/all_to_all | solution.py:57
  351.4 183.0 %psum.35 = f32[2176]{0:T(1024)S(1)} all-reduce(f32[2176]{0:T(1024)S(1)} %convert_reduce_fusion), channel_id=1, replica_groups=mesh['dp'=16,'expert'=8] {'dp'}, use_global_device_ids=true, to_apply=%region_11.13 | all-reduce | flops 2176 | bytes 17408 | tf_op jit(solution)/shard_map/psum | solution.py:115
  535.0 6.8 bitcast_reduce_fusion
  543.7 6.8 bitcast_reduce_fusion.1
  562.6 27.7 %all-reduce.2 = (f32[4,1280]{1,0:T(4,128)S(1)}, f32[]{:T(128)}) all-reduce(f32[4,1280]{1,0:T(4,128)S(1)} %fusion.29, f32[]{:T(128)} %fusion.28), channel_id=1, replica_groups=mesh['dp'=16,'expert'=8] {'expert'}, use_global_device_ids=true, to_apply=%region_14.16 | all-reduce | flops 5121 | bytes 40968 | tf_op jit(solution)/shard_map/psum | solution.py:117
  595.0 4.1 convolution_convert_fusion
  601.0 8.2 %convolution_convert_fusion.2 = bf16[1280,1280]{1,0:T(8,128)(2,1)} fusion(bf16[1280,1280]{1,0:T(8,128)(2,1)S(1)} %copy-done.5, bf16[1280,1280]{1,0:T(8,128)(2,1)} %copy-done.10), kind=kOutput, calls=%fused_computation.8 | convolution fusion | flops 4195942400 | bytes 9830400 | tf_op jit(solution)/shard_map/dot_general | solution.py:43
  609.2 10.1 %convolution_convert_fusion.1 = bf16[1280,1280]{1,0:T(8,128)(2,1)} fusion(bf16[1280,1280]{1,0:T(8,128)(2,1)S(1)} %copy-done.3, f32[1280,1280]{1,0:T(8,128)} %get-tuple-element.63), kind=kOutput, calls=%fused_computation.7 | convolution fusion | flops 4210688000 | bytes 13107200 | tf_op jit(solution)/shard_map/dot_general | solution.py:40
  620.9 25.1 %all-reduce.1 = (f32[4]{0:T(128)}, f32[4,1280]{1,0:T(4,128)S(1)}) all-reduce(f32[4]{0:T(128)S(1)} %get-tuple-element.64, f32[4,1280]{1,0:T(4,128)S(1)} %fusion.34), channel_id=1, replica_groups=mesh['dp'=16,'expert'=8] {'expert'}, use_global_device_ids=true, to_apply=%region_18.21 | all-reduce | flops 5124 | bytes 40992 | tf_op jit(solution)/shard_map/psum | solution.py:136
  649.8 3.7 reduce_sum.156
  656.6 21.2 %reduce-scatter.4.cloned.1.call-done = bf16[80,2176]{1,0:T(8,128)(2,1)} async-done(((bf16[1280,2176]{1,0:T(8,128)(2,1)}), bf16[80,2176]{1,0:T(8,128)(2,1)}) %reduce-scatter.4.cloned.1.call-update) | async-done | bytes 348176
  (86 shorter events, 54.0 us)
Async XLA Ops:
  7.2 177.8 %copy-start = (bf16[1280,1280]{1,0:T(8,128)(2,1)S(1)}, bf16[1280,1280]{1,0:T(8,128)(2,1)}, u32[]{:S(2)}) copy-start(bf16[1280,1280]{1,0:T(8,128)(2,1)} %param.14) | copy-start | bytes 9830404
  177.4 7.6 %copy-start.4 = (bf16[1280,1280]{1,0:T(8,128)(2,1)S(1)}, bf16[1280,1280]{1,0:T(8,128)(2,1)}, u32[]{:S(2)}) copy-start(bf16[1280,1280]{1,0:T(8,128)(2,1)} %reshape_squeeze.6) | copy-start | bytes 9830404
  194.4 1.8 copy-start.10
  211.4 6.3 copy-start.9
  211.4 129.4 %all-to-all-start.2 = ((f32[128,10,1280]{2,1,0:T(8,128)}), f32[128,10,1280]{2,1,0:T(8,128)}, u32[]{:S(2)}, u32[]{:S(2)}) async-start(f32[128,10,1280]{2,1,0:T(8,128)} %reshape.154), calls=%async_computation.2 | async-start | bytes 20971520 | tf_op jit(solution)/shard_map/all_to_all | solution.py:57
  237.5 113.6 %copy-start.8 = (s32[4,4]{1,0:T(4,128)S(1)}, s32[4,4]{1,0:T(4,128)}, u32[]{:S(2)}) copy-start(s32[4,4]{1,0:T(4,128)} %param.18) | copy-start | bytes 196
  340.8 202.9 %all-to-all-start.1 = ((f32[128,10,1280]{2,1,0:T(8,128)}), f32[128,10,1280]{2,1,0:T(8,128)}, u32[]{:S(2)}, u32[]{:S(2)}) async-start(f32[128,10,1280]{2,1,0:T(8,128)} %reshape.150), calls=%async_computation.1 | async-start | bytes 20971520 | tf_op jit(solution)/shard_map/all_to_all | solution.py:57
  351.1 326.7 %reduce-scatter.4.cloned.1.call-start = ((), (), s32[]{:S(2)}) async-start(), calls=%async_computation.4 | async-start | bytes 5918720
  554.6 2.3 copy-start.2
  556.9 5.5 copy-start.7
  562.5 32.5 %copy-start.6 = (bf16[128,1280]{1,0:T(8,128)(2,1)}, bf16[128,1280]{1,0:T(8,128)(2,1)S(1)}, u32[]{:S(2)}) copy-start(bf16[128,1280]{1,0:T(8,128)(2,1)S(1)} %add_convert_fusion.1) | copy-start | bytes 983044
  599.1 1.9 copy-start.5
  601.0 8.2 %copy-start.3 = (bf16[1280,1280]{1,0:T(8,128)(2,1)S(1)}, bf16[1280,1280]{1,0:T(8,128)(2,1)}, u32[]{:S(2)}) copy-start(bf16[1280,1280]{1,0:T(8,128)(2,1)} %reshape_squeeze.7) | copy-start | bytes 9830404
  601.0 18.3 %slice-start = ((s8[5570560]{0:T(1024)(128)(4,1)}), s8[4194304]{0:T(1024)(128)(4,1)S(1)}, s32[]{:S(2)}) async-start(s8[5570560]{0:T(1024)(128)(4,1)} %bitcast.43), calls=%async_computation.5 | async-start | bytes 8388608
  609.2 10.1 %slice-start.1 = ((s8[5570560]{0:T(1024)(128)(4,1)}), s8[1376256]{0:T(1024)(128)(4,1)S(1)}, s32[]{:S(2)}) async-start(s8[5570560]{0:T(1024)(128)(4,1)} %bitcast.43), calls=%async_computation.6 | async-start | bytes 2752512
  609.2 68.5 %copy-start.1 = (bf16[1280,1280]{1,0:T(8,128)(2,1)S(1)}, bf16[1280,1280]{1,0:T(8,128)(2,1)}, u32[]{:S(2)}) copy-start(bf16[1280,1280]{1,0:T(8,128)(2,1)} %param.14) | copy-start | bytes 9830404
Sparse Core Ops, SparseCore 0:
  599.2 78.4 reduce-scatter.3
where the time goes:
time: 692 us; the launch traced here: 685 us
  blocking collectives  325 us (47%)
  waiting for transfers between devices  124 us (18%)
  local copies, waits for them, and re-layouts  106 us (15%)
  matrix products  67.4 us (10%)
  other arithmetic  30.6 us (4%)
  starting transfers between devices  16.6 us (2%)
  between operations  14.8 us (2%)
    psum x1, blocking collectives, shards(): counts = lax.psum(jnp.sum(targets, axis=0), 'dp')  183 us
    all_to_all x2, waiting for transfers between devices, to_sources(): lax.all_to_all(partials, ('dp', 'expert'), split_axis=0, concat_axis=0, t...  103 us
    all_to_all x1, blocking collectives, to_experts(): lax.all_to_all(stacked, ('dp', 'expert'), split_axis=1, concat_axis=1, ti...  89.6 us
    slice x1, local copies, waits for them, and re-layouts, shards(): grad_rows = arrived[1].reshape(n_devices * capacity, D)  40.3 us
    psum x1, blocking collectives, shards(): lax.psum((pooled_part, jnp.sum(effective)), 'expert')  27.7 us
    psum x1, blocking collectives, shards(): lax.psum((normed_part, jnp.sum(focal_terms, axis=1)), 'expert')  25.1 us
    unnamed x2, waiting for transfers between devices  21.2 us
    all_to_all x2, starting transfers between devices, to_sources(): lax.all_to_all(partials, ('dp', 'expert'), split_axis=0, concat_axis=0, t...  16.5 us
  transfers between devices with their start and end apart: 3, of which 2 were waited for; matrix products, arithmetic and copies ran while one was open for 9% of the time, Pallas kernels for 0%

commit v1 on v0

--- a/solution.py
+++ b/solution.py
@@ -50,7 +50,15 @@
 
 
 def to_experts(stacked):
-    return lax.all_to_all(stacked, ("dp", "expert"), split_axis=1, concat_axis=1, tiled=True)
+    return jnp.concatenate(
+        lax.all_to_all(
+            jnp.stack(jnp.split(stacked, lax.axis_size(("dp", "expert")), axis=1)),
+            ("dp", "expert"),
+            0,
+            0,
+        ),
+        axis=1,
+    )
 
 
 def to_sources(partials):

time: 692 us -> 701 us (1.013)
  no operation moved by 1% of the time
where the time goes in v1:
time: 701 us; the launch traced here: 691 us
  blocking collectives  325 us (46%)
  waiting for transfers between devices  127 us (18%)
  local copies, waits for them, and re-layouts  110 us (16%)
  matrix products  67.3 us (10%)
  other arithmetic  30.6 us (4%)
  starting transfers between devices  16.6 us (2%)
  between operations  15.1 us (2%)
    psum x1, blocking collectives, shards(): counts = lax.psum(jnp.sum(targets, axis=0), 'dp')  183 us
    all_to_all x2, waiting for transfers between devices, to_sources(): lax.all_to_all(partials, ('dp', 'expert'), split_axis=0, concat_axis=0, t...  103 us
    all_to_all x1, blocking collectives, to_experts(): lax.all_to_all(jnp.stack(jnp.split(stacked, lax.axis_size(('dp', 'expert'...  89.1 us
    slice x1, local copies, waits for them, and re-layouts, shards(): grad_rows = arrived[1].reshape(n_devices * capacity, D)  40.3 us
    psum x1, blocking collectives, shards(): lax.psum((pooled_part, jnp.sum(effective)), 'expert')  27.6 us
    psum x1, blocking collectives, shards(): lax.psum((normed_part, jnp.sum(focal_terms, axis=1)), 'expert')  25 us
    unnamed x2, waiting for transfers between devices  23.4 us
    all_to_all x2, starting transfers between devices, to_sources(): lax.all_to_all(partials, ('dp', 'expert'), split_axis=0, concat_axis=0, t...  16.5 us
  transfers between devices with their start and end apart: 3, of which 2 were waited for; matrix products, arithmetic and copies ran while one was open for 9% of the time, Pallas kernels for 0%

profile of v1, /device:TPU:0, one launch (start us, length us, event | category | flops | bytes accessed | tf_op | source)
XLA Modules:
  0.0 691.1 jit_solution(14797674714174231719)
XLA Ops:
  29.6 3.8 broadcast_in_dim.16
  40.3 89.1 %all_to_all.15 = bf16[128,2,1,10,1280]{4,1,3,2,0:T(2,128)(2,1)S(1)} all-to-all(bf16[128,2,1,10,1280]{4,1,3,2,0:T(2,128)(2,1)S(1)} %constant_dynamic-update-slice_fusion), channel_id=1, replica_groups=mesh['dp'=16,'expert'=8] {'dp','expert'}, dimensions={0} | all-to-all | bytes 13107200 | tf_op jit(solution)/shard_map/all_to_all | solution.py:54
  129.4 40.3 %slice_reduce_fusion = (bf16[128,10,1280]{2,1,0:T(8,128)(2,1)}, bf16[128,10,1280]{2,1,0:T(8,128)(2,1)}) fusion(bf16[2,128,1,10,1280]{4,0,3,2,1:T(2,128)(2,1)S(1)} %bitcast.555), kind=kLoop, calls=%fused_computation.16 | loop fusion | bytes 13107200 | tf_op jit(solution)/shard_map/slice | solution.py:100
  169.7 7.0 %reshape_squeeze.7 = bf16[1280,1280]{1,0:T(8,128)(2,1)} reshape(bf16[128,10,1280]{2,1,0:T(8,128)(2,1)} %get-tuple-element.49) | data formatting | bytes 6553600 | tf_op jit(solution)/shard_map/reshape;squeeze | solution.py:100
  176.7 7.0 %reshape_squeeze.6 = bf16[1280,1280]{1,0:T(8,128)(2,1)} reshape(bf16[128,10,1280]{2,1,0:T(8,128)(2,1)} %get-tuple-element.50) | data formatting | bytes 6553600 | tf_op jit(solution)/shard_map/reshape;squeeze | solution.py:99
  183.7 7.6 %fusion.37 = f32[1280,1280]{1,0:T(8,128)S(1)} fusion(bf16[1280,1280]{1,0:T(8,128)(2,1)} %reshape_squeeze.7, bf16[1280,1280]{1,0:T(8,128)(2,1)} %param.15), kind=kOutput, calls=%fused_computation.358 | convolution fusion | flops 4194304000 | bytes 13107200 | tf_op jit(solution)/shard_map/dot_general | solution.py:36
  191.3 9.4 %fusion.6 = (bf16[1280,1280]{1,0:T(8,128)(2,1)S(1)}, f32[1280,1280]{1,0:T(8,128)}) fusion(f32[1280,1280]{1,0:T(8,128)S(1)} %fusion.37, bf16[1280,1280]{1,0:T(8,128)(2,1)S(1)} %copy-done.4, bf16[1280,1280]{1,0:T(8,128)(2,1)S(1)} %copy-done), kind=kOutput, calls=%fused_computation.15 | convolution fusion | flops 4227072000 | bytes 22937600 | tf_op jit(solution)/shard_map/dot_general | solution.py:32
  202.5 6.6 fusion.38
  209.0 8.6 %reshape.163 = f32[128,10,1280]{2,1,0:T(8,128)} reshape(f32[1280,1280]{1,0:T(8,128)} %fusion.38) | data formatting | bytes 13107200 | tf_op jit(solution)/shard_map/reshape | solution.py:126
  217.7 6.3 all-to-all-start.2
  224.0 11.2 %fusion.36 = f32[1280,1280]{1,0:T(8,128)} fusion(bf16[1280,1280]{1,0:T(8,128)(2,1)S(1)} %copy-done.9, f32[1280,1280]{1,0:T(8,128)} %get-tuple-element.63), kind=kOutput, calls=%fused_computation.357 | convolution fusion | flops 4209049600 | bytes 16384000 | tf_op jit(solution)/shard_map/dot_general | solution.py:35
  235.1 8.6 %reshape.159 = f32[128,10,1280]{2,1,0:T(8,128)} reshape(f32[1280,1280]{1,0:T(8,128)} %fusion.36) | data formatting | bytes 13107200 | tf_op jit(solution)/shard_map/reshape | solution.py:102
  243.8 103.3 %all-to-all-done.2 = f32[128,10,1280]{2,1,0:T(8,128)} async-done(((f32[128,10,1280]{2,1,0:T(8,128)}), f32[128,10,1280]{2,1,0:T(8,128)}, u32[]{:S(2)}, u32[]{:S(2)}) %all-to-all-start.2) | async-done | bytes 6553632 | tf_op jit(solution)/shard_map/all_to_all | solution.py:65
  347.1 10.3 %all-to-all-start.1 = ((f32[128,10,1280]{2,1,0:T(8,128)}), f32[128,10,1280]{2,1,0:T(8,128)}, u32[]{:S(2)}, u32[]{:S(2)}) async-start(f32[128,10,1280]{2,1,0:T(8,128)} %reshape.159), calls=%async_computation.1 | async-start | bytes 20971520 | tf_op jit(solution)/shard_map/all_to_all | solution.py:65
  357.6 183.0 %psum.35 = f32[2176]{0:T(1024)S(1)} all-reduce(f32[2176]{0:T(1024)S(1)} %convert_reduce_fusion), channel_id=1, replica_groups=mesh['dp'=16,'expert'=8] {'dp'}, use_global_device_ids=true, to_apply=%region_11.13 | all-reduce | flops 2176 | bytes 17408 | tf_op jit(solution)/shard_map/psum | solution.py:123
  541.3 6.8 bitcast_reduce_fusion
  550.0 6.8 bitcast_reduce_fusion.1
  568.9 27.6 %all-reduce.2 = (f32[4,1280]{1,0:T(4,128)S(1)}, f32[]{:T(128)}) all-reduce(f32[4,1280]{1,0:T(4,128)S(1)} %fusion.29, f32[]{:T(128)} %fusion.28), channel_id=1, replica_groups=mesh['dp'=16,'expert'=8] {'expert'}, use_global_device_ids=true, to_apply=%region_14.16 | all-reduce | flops 5121 | bytes 40968 | tf_op jit(solution)/shard_map/psum | solution.py:125
  601.2 4.1 convolution_convert_fusion
  605.4 8.0 %convolution_convert_fusion.2 = bf16[1280,1280]{1,0:T(8,128)(2,1)} fusion(bf16[1280,1280]{1,0:T(8,128)(2,1)S(1)} %copy-done.5, bf16[1280,1280]{1,0:T(8,128)(2,1)} %copy-done.10), kind=kOutput, calls=%fused_computation.8 | convolution fusion | flops 4195942400 | bytes 9830400 | tf_op jit(solution)/shard_map/dot_general | solution.py:43
  613.4 10.2 %convolution_convert_fusion.1 = bf16[1280,1280]{1,0:T(8,128)(2,1)} fusion(bf16[1280,1280]{1,0:T(8,128)(2,1)S(1)} %copy-done.3, f32[1280,1280]{1,0:T(8,128)} %get-tuple-element.63), kind=kOutput, calls=%fused_computation.7 | convolution fusion | flops 4210688000 | bytes 13107200 | tf_op jit(solution)/shard_map/dot_general | solution.py:40
  625.1 25.0 %all-reduce.1 = (f32[4]{0:T(128)}, f32[4,1280]{1,0:T(4,128)S(1)}) all-reduce(f32[4]{0:T(128)S(1)} %get-tuple-element.64, f32[4,1280]{1,0:T(4,128)S(1)} %fusion.34), channel_id=1, replica_groups=mesh['dp'=16,'expert'=8] {'expert'}, use_global_device_ids=true, to_apply=%region_18.21 | all-reduce | flops 5124 | bytes 40992 | tf_op jit(solution)/shard_map/psum | solution.py:144
  653.8 3.7 reduce_sum.156
  660.7 23.4 %reduce-scatter.4.cloned.1.call-done = bf16[80,2176]{1,0:T(8,128)(2,1)} async-done(((bf16[1280,2176]{1,0:T(8,128)(2,1)}), bf16[80,2176]{1,0:T(8,128)(2,1)}) %reduce-scatter.4.cloned.1.call-update) | async-done | bytes 348176
  (214 shorter events, 58.3 us)
Async XLA Ops:
  7.2 184.1 %copy-start = (bf16[1280,1280]{1,0:T(8,128)(2,1)S(1)}, bf16[1280,1280]{1,0:T(8,128)(2,1)}, u32[]{:S(2)}) copy-start(bf16[1280,1280]{1,0:T(8,128)(2,1)} %param.14) | copy-start | bytes 9830404
  183.7 7.6 %copy-start.4 = (bf16[1280,1280]{1,0:T(8,128)(2,1)S(1)}, bf16[1280,1280]{1,0:T(8,128)(2,1)}, u32[]{:S(2)}) copy-start(bf16[1280,1280]{1,0:T(8,128)(2,1)} %reshape_squeeze.6) | copy-start | bytes 9830404
  200.7 1.8 copy-start.10
  217.7 6.3 copy-start.9
  217.7 129.4 %all-to-all-start.2 = ((f32[128,10,1280]{2,1,0:T(8,128)}), f32[128,10,1280]{2,1,0:T(8,128)}, u32[]{:S(2)}, u32[]{:S(2)}) async-start(f32[128,10,1280]{2,1,0:T(8,128)} %reshape.163), calls=%async_computation.2 | async-start | bytes 20971520 | tf_op jit(solution)/shard_map/all_to_all | solution.py:65
  243.8 113.6 %copy-start.8 = (s32[4,4]{1,0:T(4,128)S(1)}, s32[4,4]{1,0:T(4,128)}, u32[]{:S(2)}) copy-start(s32[4,4]{1,0:T(4,128)} %param.18) | copy-start | bytes 196
  347.1 202.9 %all-to-all-start.1 = ((f32[128,10,1280]{2,1,0:T(8,128)}), f32[128,10,1280]{2,1,0:T(8,128)}, u32[]{:S(2)}, u32[]{:S(2)}) async-start(f32[128,10,1280]{2,1,0:T(8,128)} %reshape.159), calls=%async_computation.1 | async-start | bytes 20971520 | tf_op jit(solution)/shard_map/all_to_all | solution.py:65
  357.3 326.7 %reduce-scatter.4.cloned.1.call-start = ((), (), s32[]{:S(2)}) async-start(), calls=%async_computation.4 | async-start | bytes 5918720
  560.9 2.3 copy-start.2
  563.2 5.5 copy-start.7
  568.7 32.4 %copy-start.6 = (bf16[128,1280]{1,0:T(8,128)(2,1)}, bf16[128,1280]{1,0:T(8,128)(2,1)S(1)}, u32[]{:S(2)}) copy-start(bf16[128,1280]{1,0:T(8,128)(2,1)S(1)} %add_convert_fusion.1) | copy-start | bytes 983044
  601.2 4.2 copy-start.5
  605.4 8.0 %copy-start.3 = (bf16[1280,1280]{1,0:T(8,128)(2,1)S(1)}, bf16[1280,1280]{1,0:T(8,128)(2,1)}, u32[]{:S(2)}) copy-start(bf16[1280,1280]{1,0:T(8,128)(2,1)} %reshape_squeeze.7) | copy-start | bytes 9830404
  605.4 18.2 %slice-start = ((s8[5570560]{0:T(1024)(128)(4,1)}), s8[4194304]{0:T(1024)(128)(4,1)S(1)}, s32[]{:S(2)}) async-start(s8[5570560]{0:T(1024)(128)(4,1)} %bitcast.684), calls=%async_computation.5 | async-start | bytes 8388608
  613.4 10.2 %slice-start.1 = ((s8[5570560]{0:T(1024)(128)(4,1)}), s8[1376256]{0:T(1024)(128)(4,1)S(1)}, s32[]{:S(2)}) async-start(s8[5570560]{0:T(1024)(128)(4,1)} %bitcast.684), calls=%async_computation.6 | async-start | bytes 2752512
  613.4 70.7 %copy-start.1 = (bf16[1280,1280]{1,0:T(8,128)(2,1)S(1)}, bf16[1280,1280]{1,0:T(8,128)(2,1)}, u32[]{:S(2)}) copy-start(bf16[1280,1280]{1,0:T(8,128)(2,1)} %param.14) | copy-start | bytes 9830404
Sparse Core Ops, SparseCore 0:
  605.5 78.5 reduce-scatter.3
